TPU v7x, 32 devices: a whole 2x2x4 slice. The times are simulated.
32 devices in a mesh: group: 2 (over y), head: 4 (over x, core), st: 4 (over z).
Axes of the slice: x: 2, y: 2, z: 4, core: 2. Of those that a mesh axis runs over, the one named last changes fastest.
Arguments:
- qkv_rows: bfloat16 [12288, 3, 3072], P(('group', 'st'), None, 'head'), parts along dimension 0, may hold values from -6 to 6
- out_weight: bfloat16 [3072, 3072], P('head'), may hold values from -0.15625 to 0.15625
- residual: bfloat16 [12288, 3072], P(('group', 'st'), 'head'), parts along dimension 0, may hold values from -3 to 3
- source: int32 [12288], P(('group', 'st')), parts along dimension 0, may hold values from 0 to 6143, as said below
- target: int32 [12288], P(('group', 'st')), parts along dimension 0, may hold values from 0 to 6143, as said below
- window_first: int32 [12288], P(('group', 'st')), parts along dimension 0, may hold values from 0 to 5760, as said below
Outputs:
- layer_out: bfloat16 [12288, 3072], P(('group', 'st'), 'head'), parts along dimension 0
There are 2 independent parts, one for each index of `group`. A program takes and returns all parts, laid end to end along the dimension named above; an argument that names none is the same for every part. Nothing has to cross between parts.
Inputs may be any that keep to these rules, and one draw needn't show every extreme that they name: `source`: A permutation of the tokens that moves aligned tiles of 64 rows whole and in order. Tile t of every st device's shifted rows comes from the st device a fixed offset further along the axis (cyclically), the offset depending on t only; one st device sends at most 6 tiles to one st device, and exactly 6 to one of them. `target`: the inverse of source. `window_first`: windows are runs of whole aligned tiles inside one st device's 1536 shifted rows, of 384 to 1536 rows; in every draw some window fills all 1536 rows of a device.
All inputs are finite; a program needn't handle non-finite values.
Results may differ from a plain program's by a relative error of at most 0.0095.
Values may be sent and summed in bfloat16 or wider, within the bound.
A program may use at most 128 MiB of HBM per device.

v0:
```python
import math

import jax
import jax.numpy as jnp
from jax import lax
from jax.sharding import PartitionSpec as P

HD = 128
BLK = 64


def attend(shifted, window_first):
    tok_rows, three_way, feat_cols = shifted.shape
    head_group = feat_cols // HD
    queries = shifted[:, 0].reshape(tok_rows, head_group, HD)
    key_rows = shifted[:, 1].reshape(tok_rows, head_group, HD)
    value_rows = shifted[:, 2].reshape(tok_rows, head_group, HD)
    score_scale = 1.0 / math.sqrt(HD)
    block_rows = min(512, tok_rows)
    tile_count = tok_rows // BLK
    tile_first = window_first.reshape(tile_count, BLK)[:, 0]
    local_first = tile_first - tile_first[0]
    tile_pos = jnp.arange(tile_count, dtype=jnp.int32) * BLK
    after_tile = (tile_pos[None, :] > tile_pos[:, None]) & (
        tile_first[None, :] != tile_first[:, None]
    )
    tile_end = jnp.min(jnp.where(after_tile, tile_pos[None, :], tok_rows), axis=1)
    outputs = []
    for q_block in range(tok_rows // block_rows):
        row_start = q_block * block_rows
        first_block = local_first[row_start // BLK] // block_rows
        stop_block = (tile_end[(row_start + block_rows - 1) // BLK] + block_rows - 1) // block_rows
        q_rows = queries[row_start : row_start + block_rows]
        q_first = window_first[row_start : row_start + block_rows]

        def key_step(key_block, running):
            run_max, run_sum, run_acc = running
            key_start = key_block * block_rows
            k_rows = lax.dynamic_slice_in_dim(key_rows, key_start, block_rows, 0)
            v_rows = lax.dynamic_slice_in_dim(value_rows, key_start, block_rows, 0)
            k_first = lax.dynamic_slice_in_dim(window_first, key_start, block_rows, 0)
            scores = (
                jnp.einsum("phd,rhd->hpr", q_rows, k_rows, preferred_element_type=jnp.float32)
                * score_scale
            )
            same_window = (q_first[:, None] == k_first[None, :])[None]
            scores = jnp.where(same_window, scores, -1e30)
            new_max = jnp.maximum(run_max, jnp.max(scores, axis=2))
            factor = jnp.exp(run_max - new_max)
            expo = jnp.where(same_window, jnp.exp(scores - new_max[..., None]), 0.0)
            run_sum = run_sum * factor + jnp.sum(expo, axis=2)
            weights = expo.astype(jnp.bfloat16)
            run_acc = run_acc * factor[..., None] + jnp.einsum(
                "hpr,rhd->hpd", weights, v_rows, preferred_element_type=jnp.float32
            )
            return (new_max, run_sum, run_acc)

        initial = (
            jnp.full((head_group, block_rows), -1e30, jnp.float32),
            jnp.zeros((head_group, block_rows), jnp.float32),
            jnp.zeros((head_group, block_rows, HD), jnp.float32),
        )
        run_max, run_sum, run_acc = lax.fori_loop(first_block, stop_block, key_step, initial)
        result = run_acc / run_sum[..., None]
        outputs.append(
            jnp.transpose(result, (1, 0, 2)).reshape(block_rows, feat_cols).astype(jnp.bfloat16)
        )
    return jnp.concatenate(outputs, axis=0)


def on_device(qkv_rows, out_weight, residual, source, target, window_first):
    tok_rows, three_way, feat_cols = qkv_rows.shape
    row_width = three_way * feat_cols
    peer_count = lax.axis_size("st")
    tile_count = tok_rows // BLK
    capacity = max(2, (tile_count + peer_count - 1) // peer_count)
    dest_dev = target.reshape(tile_count, BLK)[:, 0] // tok_rows
    peer_ids = jnp.arange(peer_count, dtype=jnp.int32)
    to_peer = (dest_dev[:, None] == peer_ids[None, :]).astype(jnp.int32)
    send_rank = jnp.sum(to_peer * (jnp.cumsum(to_peer, axis=0) - to_peer), axis=1)
    send_slot = dest_dev * capacity + send_rank
    outgoing = jnp.zeros((peer_count * capacity, BLK, row_width), jnp.bfloat16)
    outgoing = outgoing.at[send_slot].set(qkv_rows.reshape(tile_count, BLK, row_width))
    incoming = lax.all_to_all(
        outgoing.reshape(peer_count, capacity * BLK, row_width),
        "st",
        split_axis=0,
        concat_axis=0,
        tiled=True,
    )
    src_tile = source.reshape(tile_count, BLK)[:, 0]
    src_dev = src_tile // tok_rows
    src_index = src_tile % tok_rows
    same_dev = src_dev[:, None] == src_dev[None, :]
    earlier = src_index[None, :] < src_index[:, None]
    recv_rank = jnp.sum((same_dev & earlier).astype(jnp.int32), axis=1)
    recv_slot = src_dev * capacity + recv_rank
    shifted = incoming.reshape(peer_count * capacity, BLK, row_width)[recv_slot]
    shifted = shifted.reshape(tok_rows, three_way, feat_cols)
    attended = attend(shifted, window_first)
    returning = jnp.zeros((peer_count * capacity, BLK, feat_cols), jnp.bfloat16)
    returning = returning.at[recv_slot].set(attended.reshape(tile_count, BLK, feat_cols))
    arrived = lax.all_to_all(
        returning.reshape(peer_count, capacity * BLK, feat_cols),
        "st",
        split_axis=0,
        concat_axis=0,
        tiled=True,
    )
    attn_home = arrived.reshape(peer_count * capacity, BLK, feat_cols)[send_slot].reshape(
        tok_rows, feat_cols
    )
    partial_term = jnp.dot(attn_home, out_weight, preferred_element_type=jnp.float32)
    projected = lax.psum_scatter(
        partial_term.astype(jnp.bfloat16), "head", scatter_dimension=1, tiled=True
    ).astype(jnp.float32)
    return (residual.astype(jnp.float32) + projected).astype(jnp.bfloat16)


def solution(mesh):
    placed = (
        P(("group", "st"), None, "head"),
        P("head", None),
        P(("group", "st"), "head"),
        P(("group", "st")),
        P(("group", "st")),
        P(("group", "st")),
    )
    return jax.shard_map(
        on_device, mesh=mesh, in_specs=placed, out_specs=P(("group", "st"), "head"), check_vma=False
    )
```

profile of v0, /device:TPU:0, one launch (start us, length us, event | category | flops | bytes accessed | tf_op | source)
XLA Modules:
  0.0 573.1 jit_solution(3600560568808832449)
XLA Ops:
  8.9 11.6 %copy.62 = bf16[1536,3,768]{2,1,0:T(4,128)(2,1)} copy(bf16[1536,3,768]{2,0,1:T(8,128)(2,1)} %param.12) | data formatting | bytes 14155776 | tf_op args[0]
  20.5 18.9 %reshape.214 = bf16[24,64,2304]{2,1,0:T(8,128)(2,1)} reshape(bf16[1536,3,768]{2,1,0:T(4,128)(2,1)} %copy.62) | data formatting | bytes 14155776 | tf_op jit(solution)/shard_map/reshape | solution.py:83
  43.1 17.1 %scatter_fusion = bf16[24,64,2304]{2,1,0:T(8,128)(2,1)} fusion(bf16[24,64,2304]{2,1,0:T(8,128)(2,1)} %broadcast_in_dim.95, s32[24]{0:T(128)S(1)} %fusion.50, bf16[24,64,2304]{2,1,0:T(8,128)(2,1)} %reshape.214), kind=kCustom, calls=%fused_computation.2 | custom fusion | bytes 21233760 | tf_op jit(solution)/shard_map/scatter | solution.py:83
  60.2 6.3 %all-to-all-start = ((bf16[4,384,2304]{2,1,0:T(8,128)(2,1)}), bf16[4,384,2304]{2,1,0:T(8,128)(2,1)}, u32[]{:S(2)}, u32[]{:S(2)}) async-start(bf16[4,384,2304]{2,1,0:T(8,128)(2,1)} %bitcast.97), calls=%async_computation | async-start | bytes 14155776 | tf_op jit(solution)/shard_map/all_to_all | solution.py:84
  79.4 142.9 %all-to-all-done = bf16[4,384,2304]{2,1,0:T(8,128)(2,1)} async-done(((bf16[4,384,2304]{2,1,0:T(8,128)(2,1)}), bf16[4,384,2304]{2,1,0:T(8,128)(2,1)}, u32[]{:S(2)}, u32[]{:S(2)}) %all-to-all-start) | async-done | bytes 7077920 | tf_op jit(solution)/shard_map/all_to_all | solution.py:84
  222.3 7.8 %gather_fusion = bf16[24,64,2304]{2,1,0:T(8,128)(2,1)} fusion(bf16[24,64,2304]{2,1,0:T(8,128)(2,1)} %bitcast.9, s32[1024]{0:T(1024)S(1)} %pad_clamp_fusion.1), kind=kCustom, calls=%fused_computation | custom fusion | bytes 14155872 | tf_op jit(solution)/shard_map/gather | solution.py:98
  230.1 16.3 %reshape.189 = bf16[1536,3,768]{2,1,0:T(4,128)(2,1)} reshape(bf16[24,64,2304]{2,1,0:T(8,128)(2,1)} %gather_fusion) | data formatting | bytes 14155776 | tf_op jit(solution)/shard_map/reshape | solution.py:99
  246.4 13.1 %fusion.61 = (bf16[1536,1,768]{2,1,0:T(2,128)(2,1)}, bf16[1536,1,768]{2,1,0:T(2,128)(2,1)}) fusion(bf16[1536,3,768]{2,1,0:T(4,128)(2,1)} %reshape.189), kind=kLoop, calls=%fused_computation.100 | loop fusion | bytes 9437184 | tf_op jit(solution)/shard_map/slice | solution.py:17
  259.5 4.4 fusion.60
  263.9 11.7 %copy.63 = bf16[1536,1,768]{0,2,1:T(8,128)(2,1)} copy(bf16[1536,1,768]{2,1,0:T(2,128)(2,1)} %get-tuple-element.346) | data formatting | bytes 4718592 | tf_op jit(solution)/shard_map/slice | solution.py:16
  278.6 11.7 %copy.65 = bf16[1536,1,768]{0,2,1:T(8,128)(2,1)} copy(bf16[1536,1,768]{2,1,0:T(2,128)(2,1)} %get-tuple-element.345) | data formatting | bytes 4718592 | tf_op jit(solution)/shard_map/slice | solution.py:17
  290.3 4.3 copy.68
  294.6 4.7 copy.64
  302.0 24.4 %while.42 = (s32[]{:T(128)}, f32[6,512]{1,0:T(8,128)S(1)}, f32[6,512]{1,0:T(8,128)S(1)}, f32[6,512,128]{2,1,0:T(8,128)}, s32[]{:T(128)}, /*index=5*/s32[512]{0:T...) while((s32[]{:T(128)}, f32[6,512]{1,0:T(8,128)S(1)}, ...), condition=%wide.region_8.9_spmd, body=%wide.region_5.8_spmd.sunk | while | flops 826808320 | bytes 38215928 | solution.py:63
  329.5 4.7 copy.70
  336.9 24.4 %while.43 = (s32[]{:T(128)}, f32[6,512]{1,0:T(8,128)S(1)}, f32[6,512]{1,0:T(8,128)S(1)}, f32[6,512,128]{2,1,0:T(8,128)}, s32[]{:T(128)}, /*index=5*/s32[512]{0:T...) while((s32[]{:T(128)}, f32[6,512]{1,0:T(8,128)S(1)}, ...), condition=%wide.region_12.13_spmd, body=%wide.region_9.12_spmd.sunk | while | flops 826808320 | bytes 38215928 | solution.py:63
  364.4 4.7 copy.75
  371.8 24.4 %while.44 = (s32[]{:T(128)}, f32[6,512]{1,0:T(8,128)S(1)}, f32[6,512]{1,0:T(8,128)S(1)}, f32[6,512,128]{2,1,0:T(8,128)}, s32[]{:T(128)}, /*index=5*/s32[512]{0:T...) while((s32[]{:T(128)}, f32[6,512]{1,0:T(8,128)S(1)}, ...), condition=%wide.region_16.17_spmd, body=%wide.region_13.16_spmd.sunk | while | flops 826808320 | bytes 38215928 | solution.py:63
  374.9 3.9 multiply_add_fusion.17
  383.0 3.9 multiply_add_fusion.17
  406.4 7.0 %scatter_fusion.1 = bf16[24,64,768]{2,1,0:T(8,128)(2,1)} fusion(bf16[24,64,768]{2,1,0:T(8,128)(2,1)} %broadcast_in_dim.93, s32[24]{0:T(128)S(1)} %copy-done.13, bf16[24,64,768]{2,1,0:T(8,128)(2,1)S(1)} %bitcast.98), kind=kCustom, calls=%fused_computation.3 | custom fusion | bytes 7077984 | tf_op jit(solution)/shard_map/scatter | solution.py:102
  417.0 53.4 %all-to-all-done.1 = bf16[4,384,768]{2,1,0:T(8,128)(2,1)S(1)} async-done(((bf16[4,384,768]{2,1,0:T(8,128)(2,1)}), bf16[4,384,768]{2,1,0:T(8,128)(2,1)S(1)}, u32[]{:S(2)}, u32[]{:S(2)}) %all-to-all-start.1) | async-done | bytes 2359328 | tf_op jit(solution)/shard_map/all_to_all | solution.py:103
  472.7 12.4 %convolution_convert_fusion = bf16[1536,3072]{1,0:T(8,128)(2,1)} fusion(bf16[1536,768]{1,0:T(8,128)(2,1)} %bitcast.108, bf16[768,3072]{1,0:T(8,128)(2,1)} %param.13), kind=kOutput, calls=%fused_computation.61 | convolution fusion | flops 7252475904 | bytes 16515072 | tf_op jit(solution)/shard_map/dot_general | solution.py:113
  485.0 77.5 %reduce-scatter.2.cloned.1.call-done = bf16[1536,768]{1,0:T(8,128)(2,1)} async-done(((bf16[1536,3072]{1,0:T(8,128)(2,1)}), bf16[1536,768]{1,0:T(8,128)(2,1)}) %reduce-scatter.2.cloned.1.call-update) | async-done | bytes 2359312 | tf_op jit(solution)/shard_map/reduce_scatter | solution.py:114
  (174 shorter events, 111.1 us)
Async XLA Ops:
  8.9 34.2 %copy-start.10 = (s32[24]{0:T(128)}, s32[24]{0:T(128)S(1)}, u32[]{:S(2)}) copy-start(s32[24]{0:T(128)S(1)} %fusion.50) | copy-start | bytes 292
  60.2 6.3 %copy-start.9 = (s32[1536]{0:T(1024)S(1)}, s32[1536]{0:T(1024)}, u32[]{:S(2)}) copy-start(s32[1536]{0:T(1024)} %param.17) | copy-start | bytes 18436
  60.2 162.1 %all-to-all-start = ((bf16[4,384,2304]{2,1,0:T(8,128)(2,1)}), bf16[4,384,2304]{2,1,0:T(8,128)(2,1)}, u32[]{:S(2)}, u32[]{:S(2)}) async-start(bf16[4,384,2304]{2,1,0:T(8,128)(2,1)} %bitcast.97), calls=%async_computation | async-start | bytes 14155776 | tf_op jit(solution)/shard_map/all_to_all | solution.py:84
  79.3 150.7 %copy-start.12 = (s32[24]{0:T(128)}, s32[24]{0:T(128)S(1)}, u32[]{:S(2)}) copy-start(s32[24]{0:T(128)S(1)} %fusion.49) | copy-start | bytes 292
  246.4 13.1 %copy-start = (bf16[1536,3,768]{2,1,0:T(4,128)(2,1)S(1)}, bf16[1536,3,768]{2,1,0:T(4,128)(2,1)}, u32[]{:S(2)}) copy-start(bf16[1536,3,768]{2,1,0:T(4,128)(2,1)} %reshape.189) | copy-start | bytes 21233668
  303.5 1.6 copy-start.4
  309.0 1.1 copy-start.5
  311.6 1.6 copy-start.4
  317.1 1.1 copy-start.5
  319.8 1.6 copy-start.4
  325.3 1.1 copy-start.5
  338.4 1.6 copy-start.6
  346.5 1.6 copy-start.6
  352.0 1.1 copy-start.7
  354.7 1.6 copy-start.6
  373.3 1.6 copy-start.2
  381.4 1.6 copy-start.2
  389.6 1.6 copy-start.2
  396.2 3.6 copy-start.1
  401.8 4.5 copy-start.13
  406.4 10.7 %copy-start.11 = (s32[24]{0:T(128)S(1)}, s32[24]{0:T(128)}, u32[]{:S(2)}) copy-start(s32[24]{0:T(128)} %copy-done.10) | copy-start | bytes 292
  413.3 57.2 %all-to-all-start.1 = ((bf16[4,384,768]{2,1,0:T(8,128)(2,1)}), bf16[4,384,768]{2,1,0:T(8,128)(2,1)S(1)}, u32[]{:S(2)}, u32[]{:S(2)}) async-start(bf16[4,384,768]{2,1,0:T(8,128)(2,1)} %bitcast.26), calls=%async_computation.1 | async-start | bytes 4718592 | tf_op jit(solution)/shard_map/all_to_all | solution.py:103
  417.0 145.6 %reduce-scatter.2.cloned.1.call-start = ((), (), s32[]{:S(2)}) async-start(), calls=%async_computation.3 | async-start | bytes 11796480 | tf_op jit(solution)/shard_map/reduce_scatter | solution.py:114
  485.0 77.5 %copy-start.8 = (bf16[1536,768]{1,0:T(8,128)(2,1)S(1)}, bf16[1536,768]{1,0:T(8,128)(2,1)}, u32[]{:S(2)}) copy-start(bf16[1536,768]{1,0:T(8,128)(2,1)} %param.14) | copy-start | bytes 7077892
  (5 other events, 5.7 us)
Sparse Core Ops, SparseCore 0:
  485.2 77.3 reduce-scatter.1
where the time goes:
time: 576 us; the launch traced here: 573 us
  waiting for transfers between devices  274 us (48%)
  local copies, waits for them, and re-layouts  182 us (32%)
  matrix products  58.3 us (10%)
  other arithmetic  24.9 us (4%)
  between operations  23.2 us (4%)
  starting transfers between devices  9.95 us (2%)
    all_to_all x1, waiting for transfers between devices, on_device(): lax.all_to_all(outgoing.reshape(peer_count, capacity * BLK, row_width), '...  143 us
    reduce_scatter x1, waiting for transfers between devices, on_device(): lax.psum_scatter(partial_term.astype(jnp.bfloat16), 'head', scatter_dimen...  77.5 us
    all_to_all x1, waiting for transfers between devices, on_device(): lax.all_to_all(returning.reshape(peer_count, capacity * BLK, feat_cols),...  53.4 us
    dot_general x9, matrix products, key_step(): jnp.einsum('hpr,rhd->hpd', weights, v_rows, preferred_element_type=jnp.fl...  35.2 us
    slice x2, local copies, waits for them, and re-layouts, attend(): value_rows = shifted[:, 2].reshape(tok_rows, head_group, HD)  24.8 us
    while x8, local copies, waits for them, and re-layouts, attend(): lax.fori_loop(first_block, stop_block, key_step, initial)  19.9 us
    reshape x1, local copies, waits for them, and re-layouts, on_device(): qkv_rows.reshape(tile_count, BLK, row_width)  18.9 us
    slice x4, local copies, waits for them, and re-layouts, attend(): q_rows = queries[row_start:row_start + block_rows]  18.4 us
  transfers between devices with their start and end apart: 3, of which 3 were waited for; matrix products, arithmetic and copies ran while one was open for 1% of the time, Pallas kernels for 0%

commit v1 on v0

v1 whole, which is shorter than its diff:
```python
import functools
import math

import jax
import jax.numpy as jnp
from jax import lax
from jax.experimental import pallas as pl
from jax.experimental.pallas import tpu as pltpu
from jax.sharding import PartitionSpec as P

HD = 128
BLK = 64
FAR = 16384.0
MESH = pl.DeviceIdType.MESH


def layer_kernel(
    dims,
    order_ref,
    wid_ref,
    slot_ref,
    qkv_ref,
    w_ref,
    out_ref,
    qbuf0,
    qbuf1,
    packed,
    recv,
    att,
    home,
    wbuf,
    acc,
    q_tag,
    k_tag,
    load_sem,
    wl_sem,
    qs,
    qr,
    rs,
    rr,
    gs,
    gr,
    ws,
    wr,
):
    n_st, n_head, heads, tiles, cap, cols = dims
    rows = cap * BLK
    total = n_st * rows
    my_st = lax.axis_index("st")
    my_head = lax.axis_index("head")

    def st_peer(step):
        return {"st": lax.rem(my_st + step + n_st, n_st)}

    def head_peer(step):
        return {"head": lax.rem(my_head + step + n_head, n_head)}

    qbufs = (qbuf0, qbuf1)

    def load_copy(j, side):
        return pltpu.make_async_copy(
            qkv_ref.at[:, :, :, pl.ds(pl.multiple_of(j * HD, HD), HD)],
            qbufs[side],
            load_sem.at[side],
        )

    def send_copy(j, step):
        part = pl.ds(step * rows, rows)
        return pltpu.make_async_remote_copy(
            src_ref=packed.at[j, :, part, :],
            dst_ref=recv.at[j, :, part, :],
            send_sem=qs.at[j, step - 1],
            recv_sem=qr.at[j, step - 1],
            device_id=st_peer(step),
            device_id_type=MESH,
        )

    def return_copy(j, step):
        part = pl.ds(step * rows, rows)
        return pltpu.make_async_remote_copy(
            src_ref=att.at[j, part, :],
            dst_ref=home.at[j, part, pl.ds(0, HD)],
            send_sem=rs.at[j, step - 1],
            recv_sem=rr.at[j, step - 1],
            device_id=st_peer(-step),
            device_id_type=MESH,
        )

    def gather_copy(j, step):
        return pltpu.make_async_remote_copy(
            src_ref=home.at[j, :, pl.ds(0, HD)],
            dst_ref=home.at[j, :, pl.ds(step * HD, HD)],
            send_sem=gs.at[j, step - 1],
            recv_sem=gr.at[j, step - 1],
            device_id=head_peer(step),
            device_id_type=MESH,
        )

    def weight_cols(step):
        owner = lax.rem(my_head + step, n_head)
        return w_ref.at[:, :, pl.ds(pl.multiple_of(owner * cols, HD), cols)]

    def weight_copy(step):
        return pltpu.make_async_remote_copy(
            src_ref=weight_cols(step),
            dst_ref=wbuf.at[:, pl.ds(step * HD, HD), :],
            send_sem=ws.at[step - 1],
            recv_sem=wr.at[step - 1],
            device_id=head_peer(step),
            device_id_type=MESH,
        )

    own_weight = pltpu.make_async_copy(weight_cols(0), wbuf.at[:, pl.ds(0, HD), :], wl_sem)

    def pack(j, side):
        load_copy(j, side).wait()
        qbuf = qbufs[side]

        def own_tile(s, carry):
            tile = order_ref[s]
            for part in range(3):
                recv[j, part, pl.ds(pl.multiple_of(s * BLK, BLK), BLK), :] = qbuf[part, tile]
            return carry

        def away_tile(s, carry):
            tile = order_ref[s]
            for part in range(3):
                packed[j, part, pl.ds(pl.multiple_of(s * BLK, BLK), BLK), :] = qbuf[part, tile]
            return carry

        lax.fori_loop(0, cap, own_tile, 0)
        lax.fori_loop(cap, n_st * cap, away_tile, 0)

    def send(j):
        for step in range(1, n_st):
            send_copy(j, step).start()

    depth = min(2, heads)
    for j in range(depth):
        load_copy(j, j % 2).start()
    own_weight.start()

    barrier = pltpu.get_barrier_semaphore()
    for step in range(1, n_st):
        pl.semaphore_signal(barrier, inc=1, device_id=st_peer(step), device_id_type=MESH)
    for step in range(1, n_head):
        pl.semaphore_signal(barrier, inc=1, device_id=head_peer(step), device_id_type=MESH)

    pack(0, 0)
    pl.semaphore_wait(barrier, n_st + n_head - 2)
    send(0)
    for j in range(1, depth):
        pack(j, j % 2)
        send(j)
    for step in range(1, n_head):
        weight_copy(step).start()
    for j in range(depth, min(depth + 2, heads)):
        load_copy(j, j % 2).start()

    lane = lax.broadcasted_iota(jnp.int32, (BLK, HD), 1)

    def tag(s, carry):
        hit = lane == wid_ref[s]
        at = pl.ds(pl.multiple_of(s * BLK, BLK), BLK)
        q_tag[at, :] = jnp.where(hit, 1.0, 0.0).astype(jnp.bfloat16)
        k_tag[at, :] = jnp.where(hit, 0.0, -FAR).astype(jnp.bfloat16)
        return carry

    lax.fori_loop(0, n_st * cap, tag, 0)
    scale = math.log2(math.e) / math.sqrt(HD)
    q_rows = 256

    def attend(j):
        def q_step(block, carry):
            at = pl.ds(pl.multiple_of(block * q_rows, q_rows), q_rows)
            q = jnp.concatenate([recv[j, 0, at, :], q_tag[at, :]], axis=1)
            k = jnp.concatenate([recv[j, 1], k_tag[...]], axis=1)
            v = jnp.concatenate([recv[j, 2], jnp.ones((total, HD), jnp.bfloat16)], axis=1)
            scores = lax.dot_general(
                q, k, (((1,), (1,)), ((), ())), preferred_element_type=jnp.float32
            )
            row_max = jnp.max(scores, axis=1, keepdims=True)
            weights = jnp.exp2((scores - row_max) * scale).astype(jnp.bfloat16)
            both = jnp.dot(weights, v, preferred_element_type=jnp.float32)
            att[j, at, :] = (both[:, :HD] / both[:, HD:]).astype(jnp.bfloat16)
            return carry

        lax.fori_loop(0, total // q_rows, q_step, 0)
        home[j, pl.ds(0, rows), pl.ds(0, HD)] = att[j, pl.ds(0, rows), :]

    def project(j):
        def row_step(block, carry):
            at = pl.ds(pl.multiple_of(block * rows, rows), rows)
            term = jnp.dot(home[j, at, :], wbuf[j], preferred_element_type=jnp.float32)
            acc[pl.ds(block * cap, cap)] += term.reshape(cap, BLK, cols)
            return carry

        lax.fori_loop(0, n_st, row_step, 0)

    acc[...] = jnp.zeros_like(acc)

    def pipeline(t, carry):
        for side in range(2):

            @pl.when((t + depth < heads) & (lax.rem(t + depth, 2) == side))
            def _():
                pack(t + depth, side)
                send(t + depth)

                @pl.when(t + depth + 2 < heads)
                def _():
                    load_copy(t + depth + 2, side).start()

        @pl.when(t < heads)
        def _():
            for step in range(1, n_st):
                send_copy(t, step).wait_recv()
            attend(t)
            for step in range(1, n_st):
                return_copy(t, step).start()

        @pl.when((t >= 1) & (t <= heads))
        def _():
            for step in range(1, n_st):
                return_copy(t - 1, step).wait_recv()
            for step in range(1, n_head):
                gather_copy(t - 1, step).start()

        @pl.when(t == 2)
        def _():
            own_weight.wait()
            for step in range(1, n_head):
                weight_copy(step).wait()

        @pl.when(t >= 2)
        def _():
            for step in range(1, n_head):
                gather_copy(t - 2, step).wait_recv()
            project(t - 2)

        return carry

    lax.fori_loop(0, heads + 2, pipeline, 0)

    def put(t, carry):
        out_ref[t] = acc[slot_ref[t]].astype(jnp.bfloat16)
        return carry

    lax.fori_loop(0, tiles, put, 0)

    def drain(j, carry):
        for step in range(1, n_st):
            send_copy(j, step).wait_send()
            return_copy(j, step).wait_send()
        for step in range(1, n_head):
            gather_copy(j, step).wait_send()
        return carry

    lax.fori_loop(0, heads, drain, 0)


def on_device(qkv_rows, out_weight, residual, source, target, window_first):
    tok_rows, three_way, feat_cols = qkv_rows.shape
    width = out_weight.shape[1]
    n_st = lax.axis_size("st")
    n_head = lax.axis_size("head")
    me = lax.axis_index("st")
    heads = feat_cols // HD
    cols = width // n_head
    tiles = tok_rows // BLK
    cap = max(2, (tiles + n_st - 1) // n_st)
    slots = n_st * cap
    total = slots * BLK

    ids = jnp.arange(tiles, dtype=jnp.int32)
    slot_ids = jnp.arange(slots, dtype=jnp.int32)
    send_block = (target.reshape(tiles, BLK)[:, 0] // tok_rows - me + n_st) % n_st
    send_rank = jnp.sum(
        ((send_block[:, None] == send_block[None, :]) & (ids[None, :] < ids[:, None])).astype(jnp.int32),
        axis=1,
    )
    send_slot = send_block * cap + send_rank
    order = jnp.sum(jnp.where(send_slot[None, :] == slot_ids[:, None], ids[None, :], 0), axis=1)
    src = source.reshape(tiles, BLK)[:, 0]
    src_block = (me - src // tok_rows + n_st) % n_st
    recv_rank = jnp.sum(
        ((src_block[:, None] == src_block[None, :]) & (src[None, :] < src[:, None])).astype(jnp.int32),
        axis=1,
    )
    recv_slot = src_block * cap + recv_rank
    window = window_first.reshape(tiles, BLK)[:, 0] // BLK - me * tiles
    wid = HD - 1 + jnp.sum(
        jnp.where(recv_slot[None, :] == slot_ids[:, None], window[None, :] - (HD - 1), 0), axis=1
    )

    dims = (n_st, n_head, heads, tiles, cap, cols)
    bf16 = jnp.bfloat16
    dma = pltpu.SemaphoreType.DMA
    smem = pl.BlockSpec(memory_space=pltpu.SMEM)
    hbm = pl.BlockSpec(memory_space=pl.ANY)
    projected = pl.pallas_call(
        functools.partial(layer_kernel, dims),
        out_shape=jax.ShapeDtypeStruct((tiles, BLK, cols), bf16),
        in_specs=[smem, smem, smem, hbm, hbm],
        out_specs=pl.BlockSpec(memory_space=pltpu.VMEM),
        scratch_shapes=[
            pltpu.VMEM((3, tiles, BLK, HD), bf16),
            pltpu.VMEM((3, tiles, BLK, HD), bf16),
            pltpu.VMEM((heads, 3, total, HD), bf16),
            pltpu.VMEM((heads, 3, total, HD), bf16),
            pltpu.VMEM((heads, total, HD), bf16),
            pltpu.VMEM((heads, total, n_head * HD), bf16),
            pltpu.VMEM((heads, n_head * HD, cols), bf16),
            pltpu.VMEM((slots, BLK, cols), jnp.float32),
            pltpu.VMEM((total, HD), bf16),
            pltpu.VMEM((total, HD), bf16),
            dma((2,)),
            dma,
            dma((heads, n_st - 1)),
            dma((heads, n_st - 1)),
            dma((heads, n_st - 1)),
            dma((heads, n_st - 1)),
            dma((heads, n_head - 1)),
            dma((heads, n_head - 1)),
            dma((n_head - 1,)),
            dma((n_head - 1,)),
        ],
        compiler_params=pltpu.CompilerParams(
            collective_id=0, has_side_effects=True, vmem_limit_bytes=60 * 1024 * 1024
        ),
    )(
        order.astype(jnp.int32),
        wid.astype(jnp.int32),
        send_slot.astype(jnp.int32),
        jnp.transpose(qkv_rows, (1, 0, 2)).reshape(three_way, tiles, BLK, feat_cols),
        out_weight.reshape(heads, HD, width),
    )
    projected = projected.reshape(tok_rows, cols)
    return (residual.astype(jnp.float32) + projected.astype(jnp.float32)).astype(bf16)


def solution(mesh):
    placed = (
        P(("group", "st"), None, "head"),
        P("head", None),
        P(("group", "st"), "head"),
        P(("group", "st")),
        P(("group", "st")),
        P(("group", "st")),
    )
    return jax.shard_map(
        on_device, mesh=mesh, in_specs=placed, out_specs=P(("group", "st"), "head"), check_vma=False
    )
```

time: 576 us -> 262 us (0.45)
  waiting for transfers between devices: 274 us -> 0 us
  Pallas kernels: 0 us -> 250 us
  local copies, waits for them, and re-layouts: 182 us -> 2.42 us
  matrix products: 58.3 us -> 0 us
  between operations: 23.2 us -> 0.05 us
  other arithmetic: 24.9 us -> 5.64 us
  starting transfers between devices: 9.95 us -> 0 us
    pallas_call x0 -> x1, Pallas kernels: none -> 250 us  [on_device(): pl.pallas_call(functools.partial(layer_kernel, dims), out_shape=jax.Shape...]
    all_to_all x2 -> x0, waiting for transfers between devices: 196 us -> none  [the longest x1 143 us: on_device(): lax.all_to_all(outgoing.reshape(peer_count, capacity * BLK, row_width), '...]
    reduce_scatter x1 -> x0, waiting for transfers between devices: 77.5 us -> none  [on_device(): lax.psum_scatter(partial_term.astype(jnp.bfloat16), 'head', scatter_dimen...]
    dot_general x19 -> x0, matrix products: 58.3 us -> none  [the longest x9 35.2 us: key_step(): jnp.einsum('hpr,rhd->hpd', weights, v_rows, preferred_element_type=jnp.fl...]
    slice x12 -> x1, local copies, waits for them, and re-layouts: 56.8 us -> 0.11 us  [on_device(): window = window_first.reshape(tiles, BLK)[:, 0] // BLK - me * tiles]
    reshape x5 -> x3, local copies, waits for them, and re-layouts: 36.9 us -> 2.3 us  [the longest x1 0.77 us: on_device(): window = window_first.reshape(tiles, BLK)[:, 0] // BLK - me * tiles]
    while x53 -> x0, local copies, waits for them, and re-layouts: 30.2 us -> none  [the longest x8 19.9 us: attend(): lax.fori_loop(first_block, stop_block, key_step, initial)]
    scatter x2 -> x0, local copies, waits for them, and re-layouts: 24 us -> none  [the longest x1 17.1 us: on_device(): outgoing.at[send_slot].set(qkv_rows.reshape(tile_count, BLK, row_width))]
  transfers between devices with their start and end apart: 3 -> 0, of which waited for: 3 -> 0; matrix products, arithmetic and copies ran while one was open for 1% -> 0% of each run, Pallas kernels for 0% -> 0%
where the time goes in v1:
time: 262 us; the launch traced here: 258 us
  Pallas kernels  250 us (95%)
  other arithmetic  5.64 us (2%)
    pallas_call x1, Pallas kernels, on_device(): pl.pallas_call(functools.partial(layer_kernel, dims), out_shape=jax.Shape...  250 us

profile of v1, /device:TPU:0, one launch (start us, length us, event | category | flops | bytes accessed | tf_op | source)
XLA Modules:
  0.0 258.4 jit_solution(9125347033579012612)
XLA Ops:
  0.0 0.8 reshape.145
  0.8 0.8 reshape.144
  1.5 0.2 fusion.4
  1.7 0.1 reduce
  1.8 0.2 convert_reduce_fusion.1
  2.0 0.0 copy-start.1
  2.0 0.6 select_reduce_fusion.1.order_ref
  2.7 0.2 convert_reduce_fusion
  2.9 0.8 reshape.146
  3.7 0.1 slice_reduce_fusion
  3.8 0.1 select_reduce_fusion
  3.9 0.5 broadcast_add_fusion.wid_ref
  4.4 0.0 copy-done.1
  4.4 0.0 copy-start
  4.4 250.3 %shard_map.64 = bf16[24,64,768]{2,1,0:T(8,128)(2,1)} custom-call(s32[24]{0:T(128)} %select_reduce_fusion.1.order_ref, s32[24]{0:T(128)} %broadcast_add_fusion.wid_ref, s32[24]{0:T(128)} %copy-done.1, bf16[3,24,64,768]{3,2,1,0:T(8,128)(2,1)} %bitcast.7, bf16[6,128,3072]{2,1,0:T(8,128)(2,1)} %bitcast.8), custom_call_target="tpu_custom_call" | custom-call | tf_op jit(solution)/shard_map/pallas_call | solution.py:301
  254.8 0.0 copy-done
  254.8 3.7 %fusion = bf16[1536,768]{1,0:T(8,128)(2,1)} fusion(bf16[1536,768]{1,0:T(8,128)(2,1)S(1)} %copy-done, bf16[24,64,768]{2,1,0:T(8,128)(2,1)} %shard_map.64), kind=kLoop, calls=%fused_computation.1 | loop fusion | flops 4718592 | bytes 7077888 | tf_op jit(solution)/shard_map/convert_element_type | solution.py:339
  (5 shorter events, 0.1 us)
Async XLA Ops:
  2.0 2.4 copy-start.1
  4.4 250.3 %copy-start = (bf16[1536,768]{1,0:T(8,128)(2,1)S(1)}, bf16[1536,768]{1,0:T(8,128)(2,1)}, u32[]{:S(2)}) copy-start(bf16[1536,768]{1,0:T(8,128)(2,1)} %param.8) | copy-start | bytes 7077892

commit v2 on v1

--- a/solution.py
+++ b/solution.py
@@ -11,6 +11,7 @@
 HD = 128
 BLK = 64
 FAR = 16384.0
+DEPTH = 2
 MESH = pl.DeviceIdType.MESH
 
 
@@ -52,9 +53,6 @@
     def st_peer(step):
         return {"st": lax.rem(my_st + step + n_st, n_st)}
 
-    def head_peer(step):
-        return {"head": lax.rem(my_head + step + n_head, n_head)}
-
     qbufs = (qbuf0, qbuf1)
 
     def load_copy(j, side):
@@ -86,27 +84,54 @@
             device_id_type=MESH,
         )
 
-    def gather_copy(j, step):
-        return pltpu.make_async_remote_copy(
-            src_ref=home.at[j, :, pl.ds(0, HD)],
-            dst_ref=home.at[j, :, pl.ds(step * HD, HD)],
-            send_sem=gs.at[j, step - 1],
-            recv_sem=gr.at[j, step - 1],
-            device_id=head_peer(step),
-            device_id_type=MESH,
-        )
-
-    def weight_cols(step):
-        owner = lax.rem(my_head + step, n_head)
-        return w_ref.at[:, :, pl.ds(pl.multiple_of(owner * cols, HD), cols)]
-
-    def weight_copy(step):
-        return pltpu.make_async_remote_copy(
-            src_ref=weight_cols(step),
-            dst_ref=wbuf.at[:, pl.ds(step * HD, HD), :],
-            send_sem=ws.at[step - 1],
-            recv_sem=wr.at[step - 1],
-            device_id=head_peer(step),
+    chips = n_head // 2
+    my_chip = my_head // 2
+    my_core = lax.rem(my_head, 2)
+
+    def head_of(place):
+        chip = lax.rem(my_chip + place // 2, chips)
+        core = my_core if place % 2 == 0 else 1 - my_core
+        return chip * 2 + core
+
+    def gather_copy(j, block, place):
+        at = pl.ds(pl.multiple_of(block * rows, rows), rows)
+        return pltpu.make_async_remote_copy(
+            src_ref=home.at[j, at, pl.ds(0, HD)],
+            dst_ref=home.at[j, at, pl.ds(place * HD, HD)],
+            send_sem=gs.at[j, block, place - 1],
+            recv_sem=gr.at[j, block, place - 1],
+            device_id={"head": head_of(place)},
+            device_id_type=MESH,
+        )
+
+    def relay_copy(j, block, place):
+        at = pl.ds(pl.multiple_of(block * rows, rows), rows)
+        return pltpu.make_async_remote_copy(
+            src_ref=home.at[j, at, pl.ds((place - 1) * HD, HD)],
+            dst_ref=home.at[j, at, pl.ds(place * HD, HD)],
+            send_sem=gs.at[j, block, place - 1],
+            recv_sem=gr.at[j, block, place - 1],
+            device_id={"head": head_of(1)},
+            device_id_type=MESH,
+        )
+
+    direct = [1] + list(range(2, n_head, 2))
+    relayed = list(range(3, n_head, 2))
+
+    def gather_block(j, block):
+        for place in direct:
+            gather_copy(j, block, place).start()
+
+    def weight_cols(place):
+        return w_ref.at[:, :, pl.ds(pl.multiple_of(head_of(place) * cols, HD), cols)]
+
+    def weight_copy(place):
+        return pltpu.make_async_remote_copy(
+            src_ref=weight_cols(place),
+            dst_ref=wbuf.at[:, pl.ds(place * HD, HD), :],
+            send_sem=ws.at[place - 1],
+            recv_sem=wr.at[place - 1],
+            device_id={"head": head_of(place)},
             device_id_type=MESH,
         )
 
@@ -132,11 +157,11 @@
         lax.fori_loop(cap, n_st * cap, away_tile, 0)
 
     def send(j):
-        for step in range(1, n_st):
+        for step in [n_st // 2] + [x for x in range(1, n_st) if x != n_st // 2]:
             send_copy(j, step).start()
 
-    depth = min(2, heads)
-    for j in range(depth):
+    depth = min(DEPTH, heads)
+    for j in range(min(2, heads)):
         load_copy(j, j % 2).start()
     own_weight.start()
 
@@ -144,18 +169,18 @@
     for step in range(1, n_st):
         pl.semaphore_signal(barrier, inc=1, device_id=st_peer(step), device_id_type=MESH)
     for step in range(1, n_head):
-        pl.semaphore_signal(barrier, inc=1, device_id=head_peer(step), device_id_type=MESH)
-
-    pack(0, 0)
-    pl.semaphore_wait(barrier, n_st + n_head - 2)
-    send(0)
-    for j in range(1, depth):
+        pl.semaphore_signal(barrier, inc=1, device_id={"head": head_of(step)}, device_id_type=MESH)
+
+    for j in range(depth):
         pack(j, j % 2)
+        if j == 0:
+            pl.semaphore_wait(barrier, n_st + n_head - 2)
         send(j)
-    for step in range(1, n_head):
-        weight_copy(step).start()
-    for j in range(depth, min(depth + 2, heads)):
-        load_copy(j, j % 2).start()
+        if j + 2 < heads:
+            load_copy(j + 2, j % 2).start()
+        if j == min(1, depth - 1):
+            for step in range(1, n_head):
+                weight_copy(step).start()
 
     lane = lax.broadcasted_iota(jnp.int32, (BLK, HD), 1)
 
@@ -168,39 +193,27 @@
 
     lax.fori_loop(0, n_st * cap, tag, 0)
     scale = math.log2(math.e) / math.sqrt(HD)
-    q_rows = 256
-
-    def attend(j):
-        def q_step(block, carry):
-            at = pl.ds(pl.multiple_of(block * q_rows, q_rows), q_rows)
-            q = jnp.concatenate([recv[j, 0, at, :], q_tag[at, :]], axis=1)
-            k = jnp.concatenate([recv[j, 1], k_tag[...]], axis=1)
-            v = jnp.concatenate([recv[j, 2], jnp.ones((total, HD), jnp.bfloat16)], axis=1)
-            scores = lax.dot_general(
-                q, k, (((1,), (1,)), ((), ())), preferred_element_type=jnp.float32
-            )
-            row_max = jnp.max(scores, axis=1, keepdims=True)
-            weights = jnp.exp2((scores - row_max) * scale).astype(jnp.bfloat16)
-            both = jnp.dot(weights, v, preferred_element_type=jnp.float32)
-            att[j, at, :] = (both[:, :HD] / both[:, HD:]).astype(jnp.bfloat16)
-            return carry
-
-        lax.fori_loop(0, total // q_rows, q_step, 0)
-        home[j, pl.ds(0, rows), pl.ds(0, HD)] = att[j, pl.ds(0, rows), :]
-
-    def project(j):
-        def row_step(block, carry):
-            at = pl.ds(pl.multiple_of(block * rows, rows), rows)
-            term = jnp.dot(home[j, at, :], wbuf[j], preferred_element_type=jnp.float32)
-            acc[pl.ds(block * cap, cap)] += term.reshape(cap, BLK, cols)
-            return carry
-
-        lax.fori_loop(0, n_st, row_step, 0)
+
+    def attend(j, step):
+        at = pl.ds(step * rows, rows)
+        q = jnp.concatenate([recv[j, 0, at, :], q_tag[at, :]], axis=1)
+        k = jnp.concatenate([recv[j, 1], k_tag[...]], axis=1)
+        v = jnp.concatenate([recv[j, 2], jnp.ones((total, HD), jnp.bfloat16)], axis=1)
+        scores = lax.dot_general(q, k, (((1,), (1,)), ((), ())), preferred_element_type=jnp.float32)
+        row_max = jnp.max(scores, axis=1, keepdims=True)
+        weights = jnp.exp2((scores - row_max) * scale).astype(jnp.bfloat16)
+        both = jnp.dot(weights, v, preferred_element_type=jnp.float32)
+        return (both[:, :HD] / both[:, HD:]).astype(jnp.bfloat16)
+
+    def project(j, block):
+        at = pl.ds(pl.multiple_of(block * rows, rows), rows)
+        term = jnp.dot(home[j, at, :], wbuf[j], preferred_element_type=jnp.float32)
+        acc[pl.ds(block * cap, cap)] += term.reshape(cap, BLK, cols)
 
     acc[...] = jnp.zeros_like(acc)
 
     def pipeline(t, carry):
-        for side in range(2):
+        for side in range(2 if depth < heads else 0):
 
             @pl.when((t + depth < heads) & (lax.rem(t + depth, 2) == side))
             def _():
@@ -215,16 +228,17 @@
         def _():
             for step in range(1, n_st):
                 send_copy(t, step).wait_recv()
-            attend(t)
-            for step in range(1, n_st):
+            for step in [n_st // 2] + [x for x in range(1, n_st) if x != n_st // 2]:
+                att[t, pl.ds(step * rows, rows), :] = attend(t, step)
                 return_copy(t, step).start()
+            home[t, pl.ds(0, rows), pl.ds(0, HD)] = attend(t, 0)
+            gather_block(t, 0)
 
         @pl.when((t >= 1) & (t <= heads))
         def _():
             for step in range(1, n_st):
                 return_copy(t - 1, step).wait_recv()
-            for step in range(1, n_head):
-                gather_copy(t - 1, step).start()
+                gather_block(t - 1, step)
 
         @pl.when(t == 2)
         def _():
@@ -234,9 +248,21 @@
 
         @pl.when(t >= 2)
         def _():
-            for step in range(1, n_head):
-                gather_copy(t - 2, step).wait_recv()
-            project(t - 2)
+            def relay(block, carry):
+                for place in relayed:
+                    gather_copy(t - 2, block, place - 1).wait_recv()
+                    relay_copy(t - 2, block, place).start()
+                return carry
+
+            def finish(block, carry):
+                gather_copy(t - 2, block, 1).wait_recv()
+                for place in relayed:
+                    relay_copy(t - 2, block, place).wait_recv()
+                project(t - 2, block)
+                return carry
+
+            lax.fori_loop(0, n_st, relay, 0)
+            lax.fori_loop(0, n_st, finish, 0)
 
         return carry
 
@@ -252,8 +278,11 @@
         for step in range(1, n_st):
             send_copy(j, step).wait_send()
             return_copy(j, step).wait_send()
-        for step in range(1, n_head):
-            gather_copy(j, step).wait_send()
+        for block in range(n_st):
+            for place in direct:
+                gather_copy(j, block, place).wait_send()
+            for place in relayed:
+                relay_copy(j, block, place).wait_send()
         return carry
 
     lax.fori_loop(0, heads, drain, 0)
@@ -320,8 +349,8 @@
             dma((heads, n_st - 1)),
             dma((heads, n_st - 1)),
             dma((heads, n_st - 1)),
-            dma((heads, n_head - 1)),
-            dma((heads, n_head - 1)),
+            dma((heads, n_st, n_head - 1)),
+            dma((heads, n_st, n_head - 1)),
             dma((n_head - 1,)),
             dma((n_head - 1,)),
         ],

time: 262 us -> 235 us (0.90); the launches traced: 258 us -> 235 us
  Pallas kernels: 250 us -> 227 us
    pallas_call x1, Pallas kernels: 250 us -> 227 us  [on_device(): pl.pallas_call(functools.partial(layer_kernel, dims), out_shape=jax.Shape...]
where the time goes in v2:
time: 235 us
  Pallas kernels  227 us (97%)
  other arithmetic  5.64 us (2%)
  local copies, waits for them, and re-layouts  2.42 us (1%)
    pallas_call x1, Pallas kernels, on_device(): pl.pallas_call(functools.partial(layer_kernel, dims), out_shape=jax.Shape...  227 us

profile of v2, /device:TPU:0, one launch (start us, length us, event | category | flops | bytes accessed | tf_op | source)
XLA Modules:
  0.0 234.6 jit_solution(11551344699166211685)
XLA Ops:
  0.0 0.8 reshape.145
  0.8 0.8 reshape.144
  1.5 0.2 fusion.4
  1.7 0.1 reduce
  1.8 0.2 convert_reduce_fusion.1
  2.0 0.0 copy-start.1
  2.0 0.6 select_reduce_fusion.1.order_ref
  2.7 0.2 convert_reduce_fusion
  2.9 0.8 reshape.146
  3.7 0.1 slice_reduce_fusion
  3.8 0.1 select_reduce_fusion
  3.9 0.5 broadcast_add_fusion.wid_ref
  4.4 0.0 copy-done.1
  4.4 0.0 copy-start
  4.4 226.5 %shard_map.64 = bf16[24,64,768]{2,1,0:T(8,128)(2,1)} custom-call(s32[24]{0:T(128)} %select_reduce_fusion.1.order_ref, s32[24]{0:T(128)} %broadcast_add_fusion.wid_ref, s32[24]{0:T(128)} %copy-done.1, bf16[3,24,64,768]{3,2,1,0:T(8,128)(2,1)} %bitcast.7, bf16[6,128,3072]{2,1,0:T(8,128)(2,1)} %bitcast.8), custom_call_target="tpu_custom_call" | custom-call | tf_op jit(solution)/shard_map/pallas_call | solution.py:330
  231.0 0.0 copy-done
  231.0 3.7 %fusion = bf16[1536,768]{1,0:T(8,128)(2,1)} fusion(bf16[1536,768]{1,0:T(8,128)(2,1)S(1)} %copy-done, bf16[24,64,768]{2,1,0:T(8,128)(2,1)} %shard_map.64), kind=kLoop, calls=%fused_computation.1 | loop fusion | flops 4718592 | bytes 7077888 | tf_op jit(solution)/shard_map/convert_element_type | solution.py:368
  (5 shorter events, 0.1 us)
Async XLA Ops:
  2.0 2.4 %copy-start.1 = (s32[24]{0:T(128)}, s32[24]{0:T(128)S(1)}, u32[]{:S(2)}) copy-start(s32[24]{0:T(128)S(1)} %multiply_add_fusion.1.slot_ref) | copy-start | bytes 292
  4.4 226.5 %copy-start = (bf16[1536,768]{1,0:T(8,128)(2,1)S(1)}, bf16[1536,768]{1,0:T(8,128)(2,1)}, u32[]{:S(2)}) copy-start(bf16[1536,768]{1,0:T(8,128)(2,1)} %param.8) | copy-start | bytes 7077892

commit v3 on v2

--- a/solution.py
+++ b/solution.py
@@ -22,6 +22,7 @@
     slot_ref,
     qkv_ref,
     w_ref,
+    res_ref,
     out_ref,
     qbuf0,
     qbuf1,
@@ -33,8 +34,10 @@
     acc,
     q_tag,
     k_tag,
+    res_buf,
     load_sem,
     wl_sem,
+    res_sem,
     qs,
     qr,
     rs,
@@ -62,13 +65,14 @@
             load_sem.at[side],
         )
 
-    def send_copy(j, step):
+    def send_copy(j, step, kind):
         part = pl.ds(step * rows, rows)
-        return pltpu.make_async_remote_copy(
-            src_ref=packed.at[j, :, part, :],
-            dst_ref=recv.at[j, :, part, :],
-            send_sem=qs.at[j, step - 1],
-            recv_sem=qr.at[j, step - 1],
+        which = pl.ds(1, 2) if kind else pl.ds(0, 1)
+        return pltpu.make_async_remote_copy(
+            src_ref=packed.at[j, which, part, :],
+            dst_ref=recv.at[j, which, part, :],
+            send_sem=qs.at[j, kind, step - 1],
+            recv_sem=qr.at[j, kind, step - 1],
             device_id=st_peer(step),
             device_id_type=MESH,
         )
@@ -156,14 +160,19 @@
         lax.fori_loop(0, cap, own_tile, 0)
         lax.fori_loop(cap, n_st * cap, away_tile, 0)
 
+    across = [n_st // 2] + [x for x in range(1, n_st) if x != n_st // 2]
+
     def send(j):
-        for step in [n_st // 2] + [x for x in range(1, n_st) if x != n_st // 2]:
-            send_copy(j, step).start()
+        for kind in (1, 0):
+            for step in across:
+                send_copy(j, step, kind).start()
 
     depth = min(DEPTH, heads)
     for j in range(min(2, heads)):
         load_copy(j, j % 2).start()
     own_weight.start()
+    res_load = pltpu.make_async_copy(res_ref, res_buf, res_sem)
+    res_load.start()
 
     barrier = pltpu.get_barrier_semaphore()
     for step in range(1, n_st):
@@ -227,12 +236,13 @@
         @pl.when(t < heads)
         def _():
             for step in range(1, n_st):
-                send_copy(t, step).wait_recv()
-            for step in [n_st // 2] + [x for x in range(1, n_st) if x != n_st // 2]:
+                send_copy(t, step, 1).wait_recv()
+            home[t, pl.ds(0, rows), pl.ds(0, HD)] = attend(t, 0)
+            gather_block(t, 0)
+            for step in across:
+                send_copy(t, step, 0).wait_recv()
                 att[t, pl.ds(step * rows, rows), :] = attend(t, step)
                 return_copy(t, step).start()
-            home[t, pl.ds(0, rows), pl.ds(0, HD)] = attend(t, 0)
-            gather_block(t, 0)
 
         @pl.when((t >= 1) & (t <= heads))
         def _():
@@ -268,15 +278,18 @@
 
     lax.fori_loop(0, heads + 2, pipeline, 0)
 
+    res_load.wait()
+
     def put(t, carry):
-        out_ref[t] = acc[slot_ref[t]].astype(jnp.bfloat16)
+        out_ref[t] = (res_buf[t].astype(jnp.float32) + acc[slot_ref[t]]).astype(jnp.bfloat16)
         return carry
 
     lax.fori_loop(0, tiles, put, 0)
 
     def drain(j, carry):
         for step in range(1, n_st):
-            send_copy(j, step).wait_send()
+            send_copy(j, step, 0).wait_send()
+            send_copy(j, step, 1).wait_send()
             return_copy(j, step).wait_send()
         for block in range(n_st):
             for place in direct:
@@ -303,21 +316,21 @@
 
     ids = jnp.arange(tiles, dtype=jnp.int32)
     slot_ids = jnp.arange(slots, dtype=jnp.int32)
-    send_block = (target.reshape(tiles, BLK)[:, 0] // tok_rows - me + n_st) % n_st
+    send_block = (lax.slice(target, (0,), (tok_rows,), (BLK,)) // tok_rows - me + n_st) % n_st
     send_rank = jnp.sum(
         ((send_block[:, None] == send_block[None, :]) & (ids[None, :] < ids[:, None])).astype(jnp.int32),
         axis=1,
     )
     send_slot = send_block * cap + send_rank
     order = jnp.sum(jnp.where(send_slot[None, :] == slot_ids[:, None], ids[None, :], 0), axis=1)
-    src = source.reshape(tiles, BLK)[:, 0]
+    src = lax.slice(source, (0,), (tok_rows,), (BLK,))
     src_block = (me - src // tok_rows + n_st) % n_st
     recv_rank = jnp.sum(
         ((src_block[:, None] == src_block[None, :]) & (src[None, :] < src[:, None])).astype(jnp.int32),
         axis=1,
     )
     recv_slot = src_block * cap + recv_rank
-    window = window_first.reshape(tiles, BLK)[:, 0] // BLK - me * tiles
+    window = lax.slice(window_first, (0,), (tok_rows,), (BLK,)) // BLK - me * tiles
     wid = HD - 1 + jnp.sum(
         jnp.where(recv_slot[None, :] == slot_ids[:, None], window[None, :] - (HD - 1), 0), axis=1
     )
@@ -330,7 +343,7 @@
     projected = pl.pallas_call(
         functools.partial(layer_kernel, dims),
         out_shape=jax.ShapeDtypeStruct((tiles, BLK, cols), bf16),
-        in_specs=[smem, smem, smem, hbm, hbm],
+        in_specs=[smem, smem, smem, hbm, hbm, hbm],
         out_specs=pl.BlockSpec(memory_space=pltpu.VMEM),
         scratch_shapes=[
             pltpu.VMEM((3, tiles, BLK, HD), bf16),
@@ -343,10 +356,12 @@
             pltpu.VMEM((slots, BLK, cols), jnp.float32),
             pltpu.VMEM((total, HD), bf16),
             pltpu.VMEM((total, HD), bf16),
+            pltpu.VMEM((tiles, BLK, cols), bf16),
             dma((2,)),
             dma,
-            dma((heads, n_st - 1)),
-            dma((heads, n_st - 1)),
+            dma,
+            dma((heads, 2, n_st - 1)),
+            dma((heads, 2, n_st - 1)),
             dma((heads, n_st - 1)),
             dma((heads, n_st - 1)),
             dma((heads, n_st, n_head - 1)),
@@ -363,9 +378,9 @@
         send_slot.astype(jnp.int32),
         jnp.transpose(qkv_rows, (1, 0, 2)).reshape(three_way, tiles, BLK, feat_cols),
         out_weight.reshape(heads, HD, width),
-    )
-    projected = projected.reshape(tok_rows, cols)
-    return (residual.astype(jnp.float32) + projected.astype(jnp.float32)).astype(bf16)
+        residual.reshape(tiles, BLK, cols),
+    )
+    return projected.reshape(tok_rows, cols)
 
 
 def solution(mesh):

time: 235 us -> 235 us (level)
  other arithmetic: 5.64 us -> 1.67 us
  local copies, waits for them, and re-layouts: 2.42 us -> 5.61 us
    convert_element_type x1 -> x0, other arithmetic: 3.66 us -> none  [on_device(): (residual.astype(jnp.float32) + projected.astype(jnp.float32)).astype(bf16)]
    unnamed x4 -> x3, local copies, waits for them, and re-layouts: 0.01 us -> 3.23 us
where the time goes in v3:
time: 235 us
  Pallas kernels  227 us (97%)
  local copies, waits for them, and re-layouts  5.61 us (2%)
    pallas_call x1, Pallas kernels, on_device(): pl.pallas_call(functools.partial(layer_kernel, dims), out_shape=jax.Shape...  227 us

profile of v3, /device:TPU:0, one launch (start us, length us, event | category | flops | bytes accessed | tf_op | source)
XLA Modules:
  0.0 234.5 jit_solution(5609086929445568206)
XLA Ops:
  0.0 0.8 slice.10
  0.8 0.8 slice.9
  1.6 0.2 convert_reduce_fusion
  1.8 0.2 convert_reduce_fusion.1
  2.0 0.0 copy-start
  2.0 0.6 select_reduce_fusion.1.order_ref
  2.6 0.8 slice.11
  3.5 0.1 select_reduce_fusion
  3.6 0.5 broadcast_add_fusion.wid_ref
  4.1 0.0 copy-done
  4.1 227.2 %shard_map.64 = bf16[24,64,768]{2,1,0:T(8,128)(2,1)} custom-call(s32[24]{0:T(128)} %select_reduce_fusion.1.order_ref, s32[24]{0:T(128)} %broadcast_add_fusion.wid_ref, s32[24]{0:T(128)} %copy-done, bf16[3,24,64,768]{3,2,1,0:T(8,128)(2,1)} %bitcast.7, bf16[6,128,3072]{2,1,0:T(8,128)(2,1)} %bitcast.8, bf16[24,64,768]{2,1,0:T(8,128)(2,1)} %bitcast.9), custom_call_target="tpu_custom_call" | custom-call | tf_op jit(solution)/shard_map/pallas_call | solution.py:343
  231.3 3.2 %copy.8 = bf16[1536,768]{1,0:T(8,128)(2,1)} copy(bf16[1536,768]{1,0:T(8,128)(2,1)} %bitcast.6) | data formatting | bytes 4718592
  (4 shorter events, 0.1 us)
Async XLA Ops:
  2.0 2.1 copy-start
